TPU v7x, 256 devices: a whole 4x4x8 slice. The times are simulated.
256 devices in a mesh: src: 2 (over y_lo), tx: 8 (over y_hi, x), ty: 16 (over z, core).
Axes of the slice: x: 4, y: 4 (y_hi: 2, y_lo: 2; y = y_hi * 2 + y_lo), z: 8, core: 2. Of those that a mesh axis runs over, the one named last changes fastest.
Arguments:
- orders: float32 [8, 2, 512, 512], P('src', None, 'tx', 'ty'), may hold values from -0.00390625 to 0.00390625
- offsets: int32 [8, 2], P('src'), may hold values from -8 to 7
- material: int32 [6, 2048, 2048], P(None, 'tx', 'ty'), may hold values from 0 to 3
- e_field: float32 [3, 6, 2048, 2048], P(None, None, 'tx', 'ty'), may hold values from -6 to 6
- h_field: float32 [3, 6, 2048, 2048], P(None, None, 'tx', 'ty'), may hold values from -6 to 6
Outputs:
- e_out: float32 [3, 6, 2048, 2048], P(None, None, 'tx', 'ty')
- h_out: float32 [3, 6, 2048, 2048], P(None, None, 'tx', 'ty')
All inputs are finite; a program needn't handle non-finite values.
Results may differ from a plain program's by a relative error of at most 0.0003.
Values sent between devices are 32-bit elements; how exact they have to be, the bound alone decides.
A program may use at most 128 MiB of HBM per device.

v0:
```python
import math
import jax
import jax.numpy as jnp
from jax import lax
from jax.sharding import PartitionSpec as P

STEPS = 4
ZINJ = 1
COURANT = 0.5
OMEGA = 0.7
PERMITTIVITY = (1.0, 2.6, 11.9, 2.1)
PREC = lax.Precision.HIGH
SPLIT = 32


def passed_along(block, axis, distance):
    devices = range(lax.axis_size(axis))
    route = [((i - distance) % len(devices), i) for i in devices]
    return lax.ppermute(block, axis, route)


def phase_tables(freqs, positions, length):
    product = jnp.mod(freqs[:, None] * positions[None, :], length)
    angle = product.astype(jnp.float32) * (2.0 * math.pi / length)
    return (jnp.cos(angle), jnp.sin(angle))


def base_tables(orders_n, positions, length):
    hi = jnp.arange(orders_n // SPLIT, dtype=jnp.int32) * SPLIT
    lo = jnp.arange(SPLIT, dtype=jnp.int32) - orders_n // 2
    c1, s1 = phase_tables(hi, positions, length)
    c2, s2 = phase_tables(lo, positions, length)
    cos_t = c1[:, None, :] * c2[None, :, :] - s1[:, None, :] * s2[None, :, :]
    sin_t = s1[:, None, :] * c2[None, :, :] + c1[:, None, :] * s2[None, :, :]
    return (cos_t.reshape(orders_n, -1), sin_t.reshape(orders_n, -1))


def cell_coefficient(material):
    total = jnp.zeros(material.shape, jnp.float32)
    for number in range(len(PERMITTIVITY)):
        total = total + jnp.where(material == number, COURANT / PERMITTIVITY[number], 0.0)
    return total


def fwd(field, axis):
    if axis == 0:
        zero = jnp.zeros((1,) + field.shape[1:], jnp.float32)
        return jnp.concatenate([field[1:], zero], 0) - field
    return jnp.roll(field, -1, axis) - field


def bwd(field, axis):
    if axis == 0:
        zero = jnp.zeros((1,) + field.shape[1:], jnp.float32)
        return field - jnp.concatenate([zero, field[:-1]], 0)
    return field - jnp.roll(field, 1, axis)


def injection_plane(orders, offsets, cells_x, cells_y):
    points, _, rows_kx, cols_ky = orders.shape
    n_tx = lax.axis_size("tx")
    n_ty = lax.axis_size("ty")
    full_x = cells_x * n_tx
    full_y = cells_y * n_ty
    mx = rows_kx * n_tx
    my = cols_ky * n_ty
    amp = lax.all_gather(orders, "ty", axis=3, tiled=True)
    a_re = amp[:, 0]
    a_im = amp[:, 1]
    y_pos = lax.axis_index("ty") * cells_y + jnp.arange(cells_y, dtype=jnp.int32)
    by_c, by_s = base_tables(my, y_pos, full_y)
    sy_c, sy_s = phase_tables(offsets[:, 1], y_pos, full_y)
    m_re = jnp.einsum("pkj,jy->pky", a_re, by_c, precision=PREC) - jnp.einsum(
        "pkj,jy->pky", a_im, by_s, precision=PREC
    )
    m_im = jnp.einsum("pkj,jy->pky", a_re, by_s, precision=PREC) + jnp.einsum(
        "pkj,jy->pky", a_im, by_c, precision=PREC
    )
    sy_c = sy_c[:, None, :]
    sy_s = sy_s[:, None, :]
    inner = jnp.stack([m_re * sy_c - m_im * sy_s, m_re * sy_s + m_im * sy_c], 1)
    inner = lax.all_gather(inner, "tx", axis=2, tiled=True)
    i_re = inner[:, 0]
    i_im = inner[:, 1]
    x_pos = lax.axis_index("tx") * cells_x + jnp.arange(cells_x, dtype=jnp.int32)
    bx_c, bx_s = base_tables(mx, x_pos, full_x)
    sx_c, sx_s = phase_tables(offsets[:, 0], x_pos, full_x)
    q_re = jnp.einsum("kx,pky->pxy", bx_c, i_re, precision=PREC) - jnp.einsum(
        "kx,pky->pxy", bx_s, i_im, precision=PREC
    )
    q_im = jnp.einsum("kx,pky->pxy", bx_c, i_im, precision=PREC) + jnp.einsum(
        "kx,pky->pxy", bx_s, i_re, precision=PREC
    )
    sx_c = sx_c[:, :, None]
    sx_s = sx_s[:, :, None]
    plane = jnp.stack(
        [jnp.sum(q_re * sx_c - q_im * sx_s, 0), jnp.sum(q_re * sx_s + q_im * sx_c, 0)]
    )
    return lax.psum(plane, "src")


def with_halo(stack, depth):
    ahead = passed_along(stack[:, :depth], "tx", -1)
    behind = passed_along(stack[:, -depth:], "tx", 1)
    stack = jnp.concatenate([stack, ahead, behind], 1)
    ahead = passed_along(jnp.swapaxes(stack[:, :, :depth], 1, 2), "ty", -1)
    behind = passed_along(jnp.swapaxes(stack[:, :, -depth:], 1, 2), "ty", 1)
    return jnp.concatenate([stack, jnp.swapaxes(ahead, 1, 2), jnp.swapaxes(behind, 1, 2)], 2)


def per_device(orders, offsets, material, e_field, h_field):
    layers, cells_x, cells_y = material.shape
    plane = injection_plane(orders, offsets, cells_x, cells_y)
    coefficient = cell_coefficient(material)
    stack = jnp.concatenate(
        [
            e_field.reshape(3 * layers, cells_x, cells_y),
            h_field.reshape(3 * layers, cells_x, cells_y),
            coefficient,
            plane,
        ],
        0,
    )
    ext = with_halo(stack, STEPS)
    n = 3 * layers
    e_x, e_y, e_z = (ext[i * layers : (i + 1) * layers] for i in range(3))
    h_x, h_y, h_z = (ext[n + i * layers : n + (i + 1) * layers] for i in range(3))
    coefficient = ext[2 * n : 2 * n + layers]
    plane_re = ext[2 * n + layers]
    plane_im = ext[2 * n + layers + 1]
    for step in range(STEPS):
        h_x = h_x - COURANT * (fwd(e_z, 2) - fwd(e_y, 0))
        h_y = h_y - COURANT * (fwd(e_x, 0) - fwd(e_z, 1))
        h_z = h_z - COURANT * (fwd(e_y, 1) - fwd(e_x, 2))
        e_x = e_x + coefficient * (bwd(h_z, 2) - bwd(h_y, 0))
        e_y = e_y + coefficient * (bwd(h_x, 0) - bwd(h_z, 1))
        e_z = e_z + coefficient * (bwd(h_y, 1) - bwd(h_x, 2))
        cosine = math.cos(OMEGA * (step + 1))
        sine = math.sin(OMEGA * (step + 1))
        e_x = e_x.at[ZINJ].add(COURANT * (cosine * plane_re - sine * plane_im))
        e_y = e_y.at[ZINJ].add(COURANT * (sine * plane_re + cosine * plane_im))
    crop = lambda f: f[:, :cells_x, :cells_y]
    return (
        jnp.stack([crop(e_x), crop(e_y), crop(e_z)]),
        jnp.stack([crop(h_x), crop(h_y), crop(h_z)]),
    )


def solution(mesh):
    in_specs = (
        P("src", None, "tx", "ty"),
        P("src", None),
        P(None, "tx", "ty"),
        P(None, None, "tx", "ty"),
        P(None, None, "tx", "ty"),
    )
    out_specs = (P(None, None, "tx", "ty"), P(None, None, "tx", "ty"))
    return jax.shard_map(
        per_device, mesh=mesh, in_specs=in_specs, out_specs=out_specs, check_vma=False
    )
```

profile of v0, /device:TPU:1, one launch (start us, length us, event | category | flops | bytes accessed | tf_op | source)
XLA Modules:
  0.0 297.1 jit_solution(6683656501134292388)
XLA Ops:
  7.2 1.6 copy.27
  10.9 43.5 %all-gather.3.cloned.1.call-done = f32[4,2,64,512]{2,0,1,3:T(4,128)} async-done(((f32[4,2,64,32]{2,0,1,3:T(4,128)}), f32[4,2,64,512]{2,0,1,3:T(4,128)}) %all-gather.3.cloned.1.call-update) | async-done | bytes 1048592 | tf_op jit(solution)/shard_map/all_gather | solution.py:67
  54.4 1.7 fusion.128
  60.0 56.0 %all-gather.5.cloned.1.call-done = f32[4,2,512,128]{3,2,0,1:T(8,128)} async-done(((f32[4,2,64,128]{3,2,0,1:T(8,128)}), f32[4,2,512,128]{3,2,0,1:T(8,128)}) %all-gather.5.cloned.1.call-update) | async-done | bytes 2097168 | tf_op jit(solution)/shard_map/all_gather | solution.py:82
  116.0 2.4 fusion.75
  123.7 33.4 %all-reduce.18.cloned.1.call-done = f32[2,256,128]{1,2,0:T(8,128)} async-done(((f32[2,256,128]{1,2,0:T(8,128)}), f32[2,256,128]{1,2,0:T(8,128)}) %all-reduce.18.cloned.1.call-update) | async-done | bytes 262160 | tf_op jit(solution)/shard_map/psum | solution.py:99
  159.3 4.6 %collective-permute-start = (f32[44,4,128]{2,1,0:T(4,128)S(1)}, f32[44,4,128]{2,1,0:T(4,128)S(1)}, u32[]{:S(2)}, u32[]{:S(2)}) collective-permute-start(f32[44,4,128]{2,1,0:T(4,128)S(1)} %get-tuple-element.134), channel_id=1, source_target_pairs={{16,0},{32,16},{48,32},{64,48},{80,64},{96,80},{112,96},{0,112},{1... | collective-permute-start | bytes 270344 | tf_op jit(solution)/shard_map/ppermute | solution.py:19
  165.5 5.4 %collective-permute-done.1 = f32[44,4,128]{2,1,0:T(4,128)S(1)} collective-permute-done((f32[44,4,128]{2,1,0:T(4,128)S(1)}, f32[44,4,128]{2,1,0:T(4,128)S(1)}, u32[]{:S(2)}, u32[]{:S(2)}) %collective-permute-start.1) | collective-permute-done | bytes 90144 | tf_op jit(solution)/shard_map/ppermute | solution.py:19
  170.9 2.1 pad_maximum_fusion.1
  173.0 6.2 %slice_bitcast_fusion.1 = (f32[44,4,264]{1,2,0:T(8,128)}, f32[44,4,264]{1,2,0:T(8,128)}) fusion(f32[44,264,128]{2,1,0:T(8,128)S(1)} %pad_maximum_fusion.1), kind=kLoop, calls=%fused_computation.2 | loop fusion | bytes 743424 | tf_op jit(solution)/shard_map/transpose | solution.py:106
  179.2 5.5 %copy.35 = f32[44,4,264]{2,1,0:T(4,128)} copy(f32[44,4,264]{1,2,0:T(8,128)} %get-tuple-element.132) | data formatting | bytes 371712 | tf_op jit(solution)/shard_map/transpose | solution.py:106
  184.8 2.6 collective-permute-start.2
  187.3 5.5 %copy.37 = f32[44,4,264]{2,1,0:T(4,128)} copy(f32[44,4,264]{1,2,0:T(8,128)} %get-tuple-element.133) | data formatting | bytes 371712 | tf_op jit(solution)/shard_map/transpose | solution.py:107
  194.0 4.8 %copy.36 = f32[44,4,264]{1,2,0:T(8,128)} copy(f32[44,4,264]{2,1,0:T(4,128)} %collective-permute-done.2) | data formatting | bytes 371712 | tf_op jit(solution)/shard_map/ppermute | solution.py:19
  198.8 4.9 %copy.38 = f32[44,4,264]{1,2,0:T(8,128)} copy(f32[44,4,264]{2,1,0:T(4,128)} %collective-permute-done.3) | data formatting | bytes 371712 | tf_op jit(solution)/shard_map/ppermute | solution.py:19
  203.7 7.5 %pad_maximum_fusion = f32[44,264,136]{2,1,0:T(8,128)S(1)} fusion(f32[44,264,4]{2,1,0:T(8,128)} %bitcast.125, f32[44,264,4]{2,1,0:T(8,128)} %bitcast.124, f32[44,4,128]{2,1,0:T(4,128)} %copy-done.15, f32[44,4,128]{2,1,0:T(4,128)S(1)} %collective-permute-done, f32[2,256,128]{2,1,0:T(8,128)S(1)} %copy.34, f32[6,256,128]{2,1,0:T(8,128)S(1)} %select_add_fusion, ...), kind=kLoop, calls=%fused_computation | loop fusion | flops 11058432 | bytes 12638208 | tf_op jit(solution)/shard_map/concatenate | solution.py:108
  212.3 2.5 copy-done.3
  217.1 2.7 fusion.9
  221.5 2.3 fusion.17
  227.3 1.6 slice.660
  229.0 1.7 slice.673
  232.6 4.1 %fusion.20 = (f32[6,264,136]{2,1,0:T(8,128)S(1)}, f32[6,264,136]{2,1,0:T(8,128)S(1)}, f32[6,264,136]{2,1,0:T(8,128)S(1)}) fusion(f32[6,264,136]{2,1,0:T(8,128)S(1)} %get-tuple-element.122, f32[6,264,136]{2,1,0:T(8,128)S(1)} %get-tuple-element.120, f32[6,1,136]{2,1,0:T(1,128)S(1)} %slice.659, f32[6,263,136]{2,1,0:T(8,128)S(1)} %slice.658, ...), kind=kLoop, calls=%fused_computation.42 | loop fusion | flops 4093056 | bytes 12638208 | tf_op jit(solution)/shard_map/sub | solution.py:134
  241.5 3.5 %fusion.35 = (f32[6,264,136]{2,1,0:T(8,128)S(1)}, f32[6,264,136]{2,1,0:T(8,128)S(1)}, f32[6,264,136]{2,1,0:T(8,128)S(1)}) fusion(f32[6,264,136]{2,1,0:T(8,128)S(1)} %get-tuple-element.120, f32[6,264,136]{2,1,0:T(8,128)S(1)} %get-tuple-element.147, f32[6,263,136]{2,1,0:T(8,128)S(1)} %bitcast.108, f32[6,1,136]{2,1,0:T(1,128)S(1)} %slice.677, ...), kind=kLoop, calls=%fused_computation.64 | loop fusion | flops 4093056 | bytes 13499904 | tf_op jit(solution)/shard_map/add | solution.py:136
  248.5 1.6 slice.682
  250.2 1.7 slice.695
  253.1 4.1 %fusion.38 = (f32[6,264,136]{2,1,0:T(8,128)S(1)}, f32[6,264,136]{2,1,0:T(8,128)S(1)}, f32[6,264,136]{2,1,0:T(8,128)S(1)}) fusion(f32[6,264,136]{2,1,0:T(8,128)S(1)} %get-tuple-element.147, f32[6,264,136]{2,1,0:T(8,128)S(1)} %get-tuple-element.118, f32[6,1,136]{2,1,0:T(1,128)S(1)} %slice.681, f32[6,263,136]{2,1,0:T(8,128)S(1)} %slice.680, ...), kind=kLoop, calls=%fused_computation.68 | loop fusion | flops 4093056 | bytes 12638208 | tf_op jit(solution)/shard_map/sub | solution.py:134
  263.0 3.5 %fusion.53 = (f32[6,264,136]{2,1,0:T(8,128)S(1)}, f32[6,264,136]{2,1,0:T(8,128)S(1)}, f32[6,264,136]{2,1,0:T(8,128)S(1)}) fusion(f32[6,264,136]{2,1,0:T(8,128)S(1)} %get-tuple-element.118, f32[6,264,136]{2,1,0:T(8,128)S(1)} %get-tuple-element.144, f32[6,263,136]{2,1,0:T(8,128)S(1)} %bitcast.110, f32[6,1,136]{2,1,0:T(1,128)S(1)} %slice.699, ...), kind=kLoop, calls=%fused_computation.90 | loop fusion | flops 4093056 | bytes 13499904 | tf_op jit(solution)/shard_map/add | solution.py:136
  269.6 2.3 fusion.56
  276.5 5.5 %fusion.59 = (f32[6,264,136]{2,1,0:T(8,128)}, f32[6,264,136]{2,1,0:T(8,128)}, f32[6,264,136]{2,1,0:T(8,128)}) fusion(f32[6,264,136]{2,1,0:T(8,128)S(1)} %get-tuple-element.117, f32[6,264,136]{2,1,0:T(8,128)S(1)} %get-tuple-element.141, f32[6,264,135]{2,1,0:T(8,128)S(1)} %bitcast.117, f32[6,264,1]{2,1,0:T(8,128)} %slice.706, ...), kind=kLoop, calls=%fused_computation.99 | loop fusion | flops 2585088 | bytes 10914816 | tf_op jit(solution)/shard_map/add | solution.py:135
  282.0 2.1 fusion.87
  284.1 1.6 slice_bitcast_fusion.9
  285.7 1.7 slice_bitcast_fusion.11
  (131 shorter events, 52.6 us)
Async XLA Ops:
  7.2 47.2 %all-gather.3.cloned.1.call-start = ((), (), s32[]{:S(2)}) async-start(), calls=%async_computation | async-start | bytes 2228224 | tf_op jit(solution)/shard_map/all_gather | solution.py:67
  8.9 107.1 %all-gather.5.cloned.1.call-start = ((), (), s32[]{:S(2)}) async-start(), calls=%async_computation.1 | async-start | bytes 2359296 | tf_op jit(solution)/shard_map/all_gather | solution.py:82
  56.4 1.0 copy-start.14
  59.3 97.8 %all-reduce.18.cloned.1.call-start = ((), (), s32[]{:S(2)}) async-start(), calls=%async_computation.2 | async-start | bytes 524288 | tf_op jit(solution)/shard_map/psum | solution.py:99
  116.0 2.4 copy-start.11
  121.5 36.7 %copy-start.1 = (f32[3,6,256,128]{3,2,1,0:T(8,128)S(1)}, f32[3,6,256,128]{3,2,1,0:T(8,128)}, u32[]{:S(2)}) copy-start(f32[3,6,256,128]{3,2,1,0:T(8,128)} %param.25) | copy-start | bytes 7077892
  158.1 12.8 %copy-start.2 = (f32[3,6,256,128]{3,2,1,0:T(8,128)S(1)}, f32[3,6,256,128]{3,2,1,0:T(8,128)}, u32[]{:S(2)}) copy-start(f32[3,6,256,128]{3,2,1,0:T(8,128)} %param.24) | copy-start | bytes 7077892
  159.3 6.2 %collective-permute-start = (f32[44,4,128]{2,1,0:T(4,128)S(1)}, f32[44,4,128]{2,1,0:T(4,128)S(1)}, u32[]{:S(2)}, u32[]{:S(2)}) collective-permute-start(f32[44,4,128]{2,1,0:T(4,128)S(1)} %get-tuple-element.134), channel_id=1, source_target_pairs={{16,0},{32,16},{48,32},{64,48},{80,64},{96,80},{112,96},{0,112},{1... | collective-permute-start | bytes 270344 | tf_op jit(solution)/shard_map/ppermute | solution.py:19
  163.9 7.0 %collective-permute-start.1 = (f32[44,4,128]{2,1,0:T(4,128)S(1)}, f32[44,4,128]{2,1,0:T(4,128)S(1)}, u32[]{:S(2)}, u32[]{:S(2)}) collective-permute-start(f32[44,4,128]{2,1,0:T(4,128)S(1)} %get-tuple-element.135), channel_id=1, source_target_pairs={{112,0},{0,16},{16,32},{32,48},{48,64},{64,80},{80,96},{96,112},{1... | collective-permute-start | bytes 270344 | tf_op jit(solution)/shard_map/ppermute | solution.py:19
  170.9 2.1 copy-start.15
  184.8 9.2 %collective-permute-start.2 = (f32[44,4,264]{2,1,0:T(4,128)}, f32[44,4,264]{2,1,0:T(4,128)}, u32[]{:S(2)}, u32[]{:S(2)}) collective-permute-start(f32[44,4,264]{2,1,0:T(4,128)} %copy.35), channel_id=1, source_target_pairs={{1,0},{2,1},{3,2},{4,3},{5,4},{6,5},{7,6},{8,7},{9,8},{10,9},{11,1... | collective-permute-start | bytes 557576 | tf_op jit(solution)/shard_map/ppermute | solution.py:19
  192.8 6.0 %collective-permute-start.3 = (f32[44,4,264]{2,1,0:T(4,128)}, f32[44,4,264]{2,1,0:T(4,128)}, u32[]{:S(2)}, u32[]{:S(2)}) collective-permute-start(f32[44,4,264]{2,1,0:T(4,128)} %copy.37), channel_id=1, source_target_pairs={{15,0},{0,1},{1,2},{2,3},{3,4},{4,5},{5,6},{6,7},{7,8},{8,9},{9,10... | collective-permute-start | bytes 557576 | tf_op jit(solution)/shard_map/ppermute | solution.py:19
  211.2 55.4 %copy-start = (f32[44,264,136]{2,1,0:T(8,128)}, f32[44,264,136]{2,1,0:T(8,128)S(1)}, u32[]{:S(2)}) copy-start(f32[44,264,136]{2,1,0:T(8,128)S(1)} %pad_maximum_fusion) | copy-start | bytes 18957316
  211.4 3.4 %copy-start.3 = (f32[3,6,256,128]{3,2,1,0:T(8,128)S(1)}, f32[3,6,256,128]{3,2,1,0:T(8,128)}, u32[]{:S(2)}) copy-start(f32[3,6,256,128]{3,2,1,0:T(8,128)} %param.24) | copy-start | bytes 7077892
  211.4 3.4 %copy-start.16 = (f32[44,4,128]{2,1,0:T(4,128)S(1)}, f32[44,4,128]{2,1,0:T(4,128)}, u32[]{:S(2)}) copy-start(f32[44,4,128]{2,1,0:T(4,128)} %copy-done.15) | copy-start | bytes 270340
  219.8 1.2 copy-start.7
  220.1 1.4 copy-start.13
  230.6 2.0 copy-start.8
  257.3 2.7 copy-start.4
  261.1 1.9 copy-start.5
  268.1 1.4 copy-start.6
  271.9 1.5 copy-start.9
  274.6 1.9 copy-start.10
  284.1 1.6 copy-start.12
Sparse Core Ops, SparseCore 0:
  10.4 43.9 all-gather.2
  59.4 56.5 all-gather.4
  122.3 34.6 all-reduce.17
where the time goes:
time: 298 us; the launch traced here: 297 us
  waiting for transfers between devices  140 us (47%)
  local copies, waits for them, and re-layouts  75.9 us (25%)
  other arithmetic  51.6 us (17%)
  between operations  14.4 us (5%)
  starting transfers between devices  8.49 us (3%)
  matrix products  6.93 us (2%)
    all_gather x1, waiting for transfers between devices, injection_plane(): inner = lax.all_gather(inner, 'tx', axis=2, tiled=True)  56 us
    all_gather x1, waiting for transfers between devices, injection_plane(): amp = lax.all_gather(orders, 'ty', axis=3, tiled=True)  43.5 us
    psum x1, waiting for transfers between devices, injection_plane(): return lax.psum(plane, 'src')  33.4 us
    slice x27, local copies, waits for them, and re-layouts, fwd(): return jnp.roll(field, -1, axis) - field  15.9 us
    sub x4, other arithmetic, per_device(): h_z = h_z - COURANT * (fwd(e_y, 1) - fwd(e_x, 2))  13.2 us
    transpose x2, local copies, waits for them, and re-layouts, with_halo(): ahead = passed_along(jnp.swapaxes(stack[:, :, :depth], 1, 2), 'ty', -1)  11.7 us
    unnamed x37, local copies, waits for them, and re-layouts  9.9 us
    ppermute x2, local copies, waits for them, and re-layouts, passed_along(): return lax.ppermute(block, axis, route)  9.72 us
  transfers between devices with their start and end apart: 7, of which 5 were waited for; matrix products, arithmetic and copies ran while one was open for 5% of the time, Pallas kernels for 0%

commit v1 on v0

--- a/solution.py
+++ b/solution.py
@@ -11,6 +11,11 @@
 PERMITTIVITY = (1.0, 2.6, 11.9, 2.1)
 PREC = lax.Precision.HIGH
 SPLIT = 32
+
+
+def summed_here(array, mesh_axis):
+    parts = lax.all_gather(array, mesh_axis)
+    return jnp.sum(parts, axis=0)
 
 
 def passed_along(block, axis, distance):
@@ -96,7 +101,7 @@
     plane = jnp.stack(
         [jnp.sum(q_re * sx_c - q_im * sx_s, 0), jnp.sum(q_re * sx_s + q_im * sx_c, 0)]
     )
-    return lax.psum(plane, "src")
+    return summed_here(plane, "src")
 
 
 def with_halo(stack, depth):

time: 298 us -> 270 us (0.906)
  waiting for transfers between devices: 140 us -> 106 us
  blocking collectives: 0 us -> 6.6 us
    psum x1 -> x0, waiting for transfers between devices: 33.4 us -> none  [injection_plane(): return lax.psum(plane, 'src')]
    all_gather x0 -> x1, blocking collectives: none -> 6.6 us  [summed_here(): parts = lax.all_gather(array, mesh_axis)]
    unnamed x37 -> x39, local copies, waits for them, and re-layouts: 9.9 us -> 9.93 us
  transfers between devices with their start and end apart: 7 -> 6, of which waited for: 5 -> 4; matrix products, arithmetic and copies ran while one was open for 5% -> 5% of each run, Pallas kernels for 0% -> 0%
where the time goes in v1:
time: 270 us; the launch traced here: 269 us
  waiting for transfers between devices  106 us (39%)
  local copies, waits for them, and re-layouts  75.9 us (28%)
  other arithmetic  51.5 us (19%)
  between operations  14.7 us (5%)
  starting transfers between devices  7.72 us (3%)
  matrix products  6.92 us (3%)
  blocking collectives  6.6 us (2%)
    all_gather x1, waiting for transfers between devices, injection_plane(): inner = lax.all_gather(inner, 'tx', axis=2, tiled=True)  55.8 us
    all_gather x1, waiting for transfers between devices, injection_plane(): amp = lax.all_gather(orders, 'ty', axis=3, tiled=True)  43.5 us
    slice x27, local copies, waits for them, and re-layouts, fwd(): return jnp.roll(field, -1, axis) - field  15.8 us
    sub x4, other arithmetic, per_device(): h_z = h_z - COURANT * (fwd(e_y, 1) - fwd(e_x, 2))  13.2 us
    transpose x2, local copies, waits for them, and re-layouts, with_halo(): ahead = passed_along(jnp.swapaxes(stack[:, :, :depth], 1, 2), 'ty', -1)  11.7 us
    unnamed x39, local copies, waits for them, and re-layouts  9.93 us
    ppermute x2, local copies, waits for them, and re-layouts, passed_along(): return lax.ppermute(block, axis, route)  9.72 us
    add x3, other arithmetic, per_device(): e_y = e_y + coefficient * (bwd(h_x, 0) - bwd(h_z, 1))  9.23 us
  transfers between devices with their start and end apart: 6, of which 4 were waited for; matrix products, arithmetic and copies ran while one was open for 5% of the time, Pallas kernels for 0%

profile of v1, /device:TPU:1, one launch (start us, length us, event | category | flops | bytes accessed | tf_op | source)
XLA Modules:
  0.0 269.4 jit_solution(11153340789428831952)
XLA Ops:
  7.2 1.6 copy.27
  10.9 43.5 %all-gather.4.cloned.1.call-done = f32[4,2,64,512]{2,0,1,3:T(4,128)} async-done(((f32[4,2,64,32]{2,0,1,3:T(4,128)}), f32[4,2,64,512]{2,0,1,3:T(4,128)}) %all-gather.4.cloned.1.call-update) | async-done | bytes 1048592 | tf_op jit(solution)/shard_map/all_gather | solution.py:72
  54.4 1.7 fusion.128
  60.3 55.8 %all-gather.6.cloned.1.call-done = f32[4,2,512,128]{3,2,0,1:T(8,128)} async-done(((f32[4,2,64,128]{3,2,0,1:T(8,128)}), f32[4,2,512,128]{3,2,0,1:T(8,128)}) %all-gather.6.cloned.1.call-update) | async-done | bytes 2097168 | tf_op jit(solution)/shard_map/all_gather | solution.py:87
  116.0 2.4 fusion.75
  123.3 6.6 %all-gather = f32[4,256,128]{2,1,0:T(8,128)} all-gather(f32[2,256,128]{2,1,0:T(8,128)S(1)} %copy.34), channel_id=2, replica_groups=mesh['src'=2,'tx'=8,'ty'=16] {'src'}, dimensions={0}, use_global_device_ids=true | all-gather | bytes 786432 | tf_op jit(solution)/shard_map/all_gather | solution.py:17
  133.7 1.9 collective-permute-done
  135.6 4.8 %collective-permute-done.1 = f32[44,4,128]{2,1,0:T(4,128)S(1)} collective-permute-done((f32[44,4,128]{2,1,0:T(4,128)S(1)}, f32[44,4,128]{2,1,0:T(4,128)S(1)}, u32[]{:S(2)}, u32[]{:S(2)}) %collective-permute-start.1) | collective-permute-done | bytes 90144 | tf_op jit(solution)/shard_map/ppermute | solution.py:24
  140.5 2.1 pad_maximum_fusion.1
  142.6 6.2 %slice_bitcast_fusion.1 = (f32[44,4,264]{1,2,0:T(8,128)}, f32[44,4,264]{1,2,0:T(8,128)}) fusion(f32[44,264,128]{2,1,0:T(8,128)S(1)} %pad_maximum_fusion.1), kind=kLoop, calls=%fused_computation.2 | loop fusion | bytes 743424 | tf_op jit(solution)/shard_map/transpose | solution.py:111
  148.8 5.5 %copy.35 = f32[44,4,264]{2,1,0:T(4,128)} copy(f32[44,4,264]{1,2,0:T(8,128)} %get-tuple-element.132) | data formatting | bytes 371712 | tf_op jit(solution)/shard_map/transpose | solution.py:111
  154.3 4.9 %collective-permute-start.2 = (f32[44,4,264]{2,1,0:T(4,128)}, f32[44,4,264]{2,1,0:T(4,128)}, u32[]{:S(2)}, u32[]{:S(2)}) collective-permute-start(f32[44,4,264]{2,1,0:T(4,128)} %copy.35), channel_id=1, source_target_pairs={{1,0},{2,1},{3,2},{4,3},{5,4},{6,5},{7,6},{8,7},{9,8},{10,9},{11,1... | collective-permute-start | bytes 557576 | tf_op jit(solution)/shard_map/ppermute | solution.py:24
  159.3 5.5 %copy.37 = f32[44,4,264]{2,1,0:T(4,128)} copy(f32[44,4,264]{1,2,0:T(8,128)} %get-tuple-element.133) | data formatting | bytes 371712 | tf_op jit(solution)/shard_map/transpose | solution.py:112
  165.9 4.8 %copy.36 = f32[44,4,264]{1,2,0:T(8,128)} copy(f32[44,4,264]{2,1,0:T(4,128)} %collective-permute-done.2) | data formatting | bytes 371712 | tf_op jit(solution)/shard_map/ppermute | solution.py:24
  170.8 4.9 %copy.38 = f32[44,4,264]{1,2,0:T(8,128)} copy(f32[44,4,264]{2,1,0:T(4,128)} %collective-permute-done.3) | data formatting | bytes 371712 | tf_op jit(solution)/shard_map/ppermute | solution.py:24
  175.7 7.5 %pad_maximum_fusion = f32[44,264,136]{2,1,0:T(8,128)S(1)} fusion(f32[44,264,4]{2,1,0:T(8,128)} %bitcast.126, f32[44,264,4]{2,1,0:T(8,128)} %bitcast.125, f32[44,4,128]{2,1,0:T(4,128)} %copy-done.15, f32[44,4,128]{2,1,0:T(4,128)S(1)} %collective-permute-done, f32[2,256,128]{2,1,0:T(8,128)S(1)} %reduce_sum.35, f32[6,256,128]{2,1,0:T(8,128)S(1)} %select_add_fusion, ...), kind=kLoop, calls=%fused_computation | loop fusion | flops 11058432 | bytes 12638208 | tf_op jit(solution)/shard_map/concatenate | solution.py:113
  184.3 2.5 copy-done.3
  189.1 2.7 fusion.9
  193.5 2.3 fusion.17
  199.3 1.6 slice.660
  201.0 1.6 slice.673
  204.6 4.1 %fusion.20 = (f32[6,264,136]{2,1,0:T(8,128)S(1)}, f32[6,264,136]{2,1,0:T(8,128)S(1)}, f32[6,264,136]{2,1,0:T(8,128)S(1)}) fusion(f32[6,264,136]{2,1,0:T(8,128)S(1)} %get-tuple-element.122, f32[6,264,136]{2,1,0:T(8,128)S(1)} %get-tuple-element.120, f32[6,1,136]{2,1,0:T(1,128)S(1)} %slice.659, f32[6,263,136]{2,1,0:T(8,128)S(1)} %slice.658, ...), kind=kLoop, calls=%fused_computation.42 | loop fusion | flops 4093056 | bytes 12638208 | tf_op jit(solution)/shard_map/sub | solution.py:139
  213.5 3.5 %fusion.35 = (f32[6,264,136]{2,1,0:T(8,128)S(1)}, f32[6,264,136]{2,1,0:T(8,128)S(1)}, f32[6,264,136]{2,1,0:T(8,128)S(1)}) fusion(f32[6,264,136]{2,1,0:T(8,128)S(1)} %get-tuple-element.120, f32[6,264,136]{2,1,0:T(8,128)S(1)} %get-tuple-element.147, f32[6,263,136]{2,1,0:T(8,128)S(1)} %bitcast.109, f32[6,1,136]{2,1,0:T(1,128)S(1)} %slice.677, ...), kind=kLoop, calls=%fused_computation.64 | loop fusion | flops 4093056 | bytes 13499904 | tf_op jit(solution)/shard_map/add | solution.py:141
  220.5 1.6 slice.682
  222.1 1.7 slice.695
  225.1 4.1 %fusion.38 = (f32[6,264,136]{2,1,0:T(8,128)S(1)}, f32[6,264,136]{2,1,0:T(8,128)S(1)}, f32[6,264,136]{2,1,0:T(8,128)S(1)}) fusion(f32[6,264,136]{2,1,0:T(8,128)S(1)} %get-tuple-element.147, f32[6,264,136]{2,1,0:T(8,128)S(1)} %get-tuple-element.118, f32[6,1,136]{2,1,0:T(1,128)S(1)} %slice.681, f32[6,263,136]{2,1,0:T(8,128)S(1)} %slice.680, ...), kind=kLoop, calls=%fused_computation.68 | loop fusion | flops 4093056 | bytes 12638208 | tf_op jit(solution)/shard_map/sub | solution.py:139
  235.0 3.5 %fusion.53 = (f32[6,264,136]{2,1,0:T(8,128)S(1)}, f32[6,264,136]{2,1,0:T(8,128)S(1)}, f32[6,264,136]{2,1,0:T(8,128)S(1)}) fusion(f32[6,264,136]{2,1,0:T(8,128)S(1)} %get-tuple-element.118, f32[6,264,136]{2,1,0:T(8,128)S(1)} %get-tuple-element.144, f32[6,263,136]{2,1,0:T(8,128)S(1)} %bitcast.111, f32[6,1,136]{2,1,0:T(1,128)S(1)} %slice.699, ...), kind=kLoop, calls=%fused_computation.90 | loop fusion | flops 4093056 | bytes 13499904 | tf_op jit(solution)/shard_map/add | solution.py:141
  241.5 2.3 fusion.56
  248.5 5.5 %fusion.59 = (f32[6,264,136]{2,1,0:T(8,128)}, f32[6,264,136]{2,1,0:T(8,128)}, f32[6,264,136]{2,1,0:T(8,128)}) fusion(f32[6,264,136]{2,1,0:T(8,128)S(1)} %get-tuple-element.117, f32[6,264,136]{2,1,0:T(8,128)S(1)} %get-tuple-element.141, f32[6,264,135]{2,1,0:T(8,128)S(1)} %bitcast.118, f32[6,264,1]{2,1,0:T(8,128)} %slice.706, ...), kind=kLoop, calls=%fused_computation.99 | loop fusion | flops 2585088 | bytes 10914816 | tf_op jit(solution)/shard_map/add | solution.py:140
  253.9 2.1 fusion.87
  256.0 1.6 slice_bitcast_fusion.9
  257.7 1.7 slice_bitcast_fusion.11
  (132 shorter events, 52.5 us)
Async XLA Ops:
  7.2 47.2 %all-gather.4.cloned.1.call-start = ((), (), s32[]{:S(2)}) async-start(), calls=%async_computation | async-start | bytes 2228224 | tf_op jit(solution)/shard_map/all_gather | solution.py:72
  8.9 107.1 %all-gather.6.cloned.1.call-start = ((), (), s32[]{:S(2)}) async-start(), calls=%async_computation.1 | async-start | bytes 2359296 | tf_op jit(solution)/shard_map/all_gather | solution.py:87
  56.4 1.0 copy-start.14
  58.1 1.8 copy-start.17
  116.0 2.4 copy-start.11
  121.5 9.6 %copy-start.1 = (f32[3,6,256,128]{3,2,1,0:T(8,128)S(1)}, f32[3,6,256,128]{3,2,1,0:T(8,128)}, u32[]{:S(2)}) copy-start(f32[3,6,256,128]{3,2,1,0:T(8,128)} %param.25) | copy-start | bytes 7077892
  131.1 9.4 %copy-start.2 = (f32[3,6,256,128]{3,2,1,0:T(8,128)S(1)}, f32[3,6,256,128]{3,2,1,0:T(8,128)}, u32[]{:S(2)}) copy-start(f32[3,6,256,128]{3,2,1,0:T(8,128)} %param.24) | copy-start | bytes 7077892
  132.2 3.5 %collective-permute-start = (f32[44,4,128]{2,1,0:T(4,128)S(1)}, f32[44,4,128]{2,1,0:T(4,128)S(1)}, u32[]{:S(2)}, u32[]{:S(2)}) collective-permute-start(f32[44,4,128]{2,1,0:T(4,128)S(1)} %get-tuple-element.134), channel_id=1, source_target_pairs={{16,0},{32,16},{48,32},{64,48},{80,64},{96,80},{112,96},{0,112},{1... | collective-permute-start | bytes 270344 | tf_op jit(solution)/shard_map/ppermute | solution.py:24
  133.5 7.0 %collective-permute-start.1 = (f32[44,4,128]{2,1,0:T(4,128)S(1)}, f32[44,4,128]{2,1,0:T(4,128)S(1)}, u32[]{:S(2)}, u32[]{:S(2)}) collective-permute-start(f32[44,4,128]{2,1,0:T(4,128)S(1)} %get-tuple-element.135), channel_id=1, source_target_pairs={{112,0},{0,16},{16,32},{32,48},{48,64},{64,80},{80,96},{96,112},{1... | collective-permute-start | bytes 270344 | tf_op jit(solution)/shard_map/ppermute | solution.py:24
  140.5 2.1 copy-start.15
  154.3 11.6 %collective-permute-start.2 = (f32[44,4,264]{2,1,0:T(4,128)}, f32[44,4,264]{2,1,0:T(4,128)}, u32[]{:S(2)}, u32[]{:S(2)}) collective-permute-start(f32[44,4,264]{2,1,0:T(4,128)} %copy.35), channel_id=1, source_target_pairs={{1,0},{2,1},{3,2},{4,3},{5,4},{6,5},{7,6},{8,7},{9,8},{10,9},{11,1... | collective-permute-start | bytes 557576 | tf_op jit(solution)/shard_map/ppermute | solution.py:24
  164.8 6.0 %collective-permute-start.3 = (f32[44,4,264]{2,1,0:T(4,128)}, f32[44,4,264]{2,1,0:T(4,128)}, u32[]{:S(2)}, u32[]{:S(2)}) collective-permute-start(f32[44,4,264]{2,1,0:T(4,128)} %copy.37), channel_id=1, source_target_pairs={{15,0},{0,1},{1,2},{2,3},{3,4},{4,5},{5,6},{6,7},{7,8},{8,9},{9,10... | collective-permute-start | bytes 557576 | tf_op jit(solution)/shard_map/ppermute | solution.py:24
  183.2 55.4 %copy-start = (f32[44,264,136]{2,1,0:T(8,128)}, f32[44,264,136]{2,1,0:T(8,128)S(1)}, u32[]{:S(2)}) copy-start(f32[44,264,136]{2,1,0:T(8,128)S(1)} %pad_maximum_fusion) | copy-start | bytes 18957316
  183.4 3.4 %copy-start.3 = (f32[3,6,256,128]{3,2,1,0:T(8,128)S(1)}, f32[3,6,256,128]{3,2,1,0:T(8,128)}, u32[]{:S(2)}) copy-start(f32[3,6,256,128]{3,2,1,0:T(8,128)} %param.24) | copy-start | bytes 7077892
  183.4 3.4 %copy-start.16 = (f32[44,4,128]{2,1,0:T(4,128)S(1)}, f32[44,4,128]{2,1,0:T(4,128)}, u32[]{:S(2)}) copy-start(f32[44,4,128]{2,1,0:T(4,128)} %copy-done.15) | copy-start | bytes 270340
  191.8 1.2 copy-start.7
  192.1 1.4 copy-start.13
  202.6 2.0 copy-start.8
  229.2 2.7 copy-start.4
  233.1 1.9 copy-start.5
  240.1 1.4 copy-start.6
  243.8 1.5 copy-start.9
  246.6 1.9 copy-start.10
  256.0 1.6 copy-start.12
Sparse Core Ops, SparseCore 0:
  10.4 43.9 all-gather.3
  59.4 56.5 all-gather.5
